TPU v7x, 32 devices: a whole 2x2x4 slice. The times are simulated.
32 devices in a mesh: field: 2 (over y), epoch: 4 (over z), sky: 4 (over x, core).
Axes of the slice: x: 2, y: 2, z: 4, core: 2. Of those that a mesh axis runs over, the one named last changes fastest.
Arguments:
- sky_scene: bfloat16 [4096, 2048], P(('field', 'epoch'), 'sky'), parts along dimension 0, may hold values from -6 to 6
- images: bfloat16 [16, 2048, 2048], P(('field', 'epoch'), None, 'sky'), parts along dimension 0, may hold values from -6 to 6
- psf_rows: bfloat16 [16, 25], P('field'), parts along dimension 0, may hold values from 0.0099487305 to 0.06982422
- psf_cols: bfloat16 [16, 25], P('field'), parts along dimension 0, may hold values from 0.0099487305 to 0.06982422
- offsets: int32 [16, 2], P('field'), parts along dimension 0, may hold values from -4 to 4, as said below
- epoch_weight: float32 [16], P('field'), parts along dimension 0, may hold values from 0.25 to 2
- column_mask: int32 [16, 2048], P('field', 'sky'), parts along dimension 0, may hold values 0 or 1
- coverage: int32 [16, 4, 4], P('field'), parts along dimension 0, may hold values from 0 to 1, as said below
Outputs:
- gradient: float32 [4096, 2048], P(('field', 'epoch'), 'sky'), parts along dimension 0
There are 2 independent parts, one for each index of `field`. A program takes and returns all parts, laid end to end along the dimension named above; each array names one. Nothing has to cross between parts.
Inputs may be any that keep to these rules, and one draw needn't show every extreme that they name: `offsets`: column 0 shifts rows and column 1 shifts columns. `coverage`: the tiles that one epoch covers form a rectangle of whole tiles that spans all tile rows or all but one of them, and all tile columns or all but one of them.
All inputs are finite; a program needn't handle non-finite values. No bound on the sum of `column_mask` on one device may be relied on, other than what follows from the above.
Results may differ from a plain program's by a relative error of at most 0.0045.
Values may be sent and summed in bfloat16 or wider, within the bound.
A program may use at most 64 MiB of HBM per device.

v0:
```python
import jax
import jax.numpy as jnp
from jax import lax
from jax.sharding import PartitionSpec as P

TILE = 512
HALO = 16


def extended(value, sides, width):
    for axis, dim in sides:
        peers, length = (lax.axis_size(axis), value.shape[dim])
        up = [(i, (i + 1) % peers) for i in range(peers - 1)]
        down = [(j, i) for i, j in up]
        last = lax.slice_in_dim(value, length - width, length, axis=dim)
        initial = lax.slice_in_dim(value, 0, width, axis=dim)
        before = lax.ppermute(last, axis, up)
        after = lax.ppermute(initial, axis, down)
        value = jnp.concatenate([before, value, after], axis=dim)
    return value


def band_tables(kernels, shifts, count_in, count_out):
    row_index = lax.broadcasted_iota(jnp.int32, (count_in, count_out), 0)
    col_index = lax.broadcasted_iota(jnp.int32, (count_in, count_out), 1)
    spread = kernels.shape[1]
    half_width = (spread - 1) // 2
    position = (
        (row_index - col_index)[None]
        - shifts[:, None, None]
        + half_width
        - (count_in - count_out) // 2
    )
    band_table = jnp.zeros((kernels.shape[0], count_in, count_out), jnp.float32)
    for each_tap in range(spread):
        band_table = band_table + jnp.where(
            position == each_tap, kernels[:, each_tap, None, None].astype(jnp.float32), 0.0
        )
    return band_table.astype(jnp.bfloat16)


def epoch_block(window, row_table, col_table, image_block, factor):
    lifted = jnp.einsum("ki,kc->ic", row_table, window, preferred_element_type=jnp.float32).astype(
        jnp.bfloat16
    )
    modeled = jnp.dot(lifted, col_table, preferred_element_type=jnp.float32)
    residual = (factor * (modeled - image_block.astype(jnp.float32))).astype(jnp.bfloat16)
    pulled = jnp.einsum(
        "ic,kc->ik", residual, col_table, preferred_element_type=jnp.float32
    ).astype(jnp.bfloat16)
    return jnp.dot(row_table, pulled, preferred_element_type=jnp.float32)


def strip_plan(sky_scene, images, psf_rows, psf_cols, offsets, epoch_weight, column_mask, coverage):
    slab_cells = extended(sky_scene, (("sky", 1),), HALO)
    strip_cells = lax.all_gather(slab_cells, "epoch", axis=0, tiled=True)
    strip_cells = jnp.pad(strip_cells, ((HALO, HALO), (0, 0)))
    full_rows = strip_cells.shape[0] - 2 * HALO
    strip_width = sky_scene.shape[1]
    local_count = images.shape[0]
    epoch_base = lax.axis_index("epoch") * local_count
    tile_column = lax.axis_index("sky") * strip_width // TILE

    def per_epoch(local_epoch, running):
        epoch_now = epoch_base + local_epoch
        row_table = band_tables(
            psf_rows[epoch_now][None], offsets[epoch_now, 0][None], TILE + 2 * HALO, TILE
        )[0]
        col_table = band_tables(
            psf_cols[epoch_now][None],
            offsets[epoch_now, 1][None],
            strip_width + 2 * HALO,
            strip_width,
        )[0]
        observed = lax.dynamic_index_in_dim(images, local_epoch, 0, keepdims=False)
        weight = epoch_weight[epoch_now]
        mask_row = column_mask[epoch_now].astype(jnp.float32)
        for row_block in range(full_rows // TILE):
            covered_flag = coverage[epoch_now, row_block, tile_column]
            window = strip_cells[row_block * TILE : row_block * TILE + TILE + 2 * HALO]
            image_block = observed[row_block * TILE : (row_block + 1) * TILE]
            factor = 2.0 * weight * covered_flag.astype(jnp.float32) * mask_row

            def covered():
                return epoch_block(window, row_table, col_table, image_block, factor)

            def skipped():
                return jnp.zeros((TILE + 2 * HALO, strip_width + 2 * HALO), jnp.float32)

            grad_term = lax.cond(covered_flag > 0, covered, skipped)
            running = running.at[row_block * TILE : row_block * TILE + TILE + 2 * HALO].add(
                grad_term
            )
        return running

    running = lax.fori_loop(
        0,
        local_count,
        per_epoch,
        jnp.zeros((full_rows + 2 * HALO, strip_width + 2 * HALO), jnp.float32),
    )
    trimmed = running[HALO : HALO + full_rows]
    packed = jnp.concatenate([trimmed[:, :HALO], trimmed[:, strip_width + HALO :]], axis=1)
    center_raw = trimmed[:, HALO : HALO + strip_width]
    received = extended(packed, (("sky", 1),), HALO)
    center_cells = center_raw.at[:, :HALO].add(received[:, :HALO])
    center_cells = center_cells.at[:, strip_width - HALO :].add(received[:, 3 * HALO :])
    return lax.psum_scatter(center_cells, "epoch", scatter_dimension=0, tiled=True)


def on_device(sky_scene, images, psf_rows, psf_cols, offsets, epoch_weight, column_mask, coverage):
    return strip_plan(
        sky_scene, images, psf_rows, psf_cols, offsets, epoch_weight, column_mask, coverage
    )


def solution(mesh):
    return jax.shard_map(
        on_device,
        mesh=mesh,
        in_specs=(
            P(("field", "epoch"), "sky"),
            P(("field", "epoch"), None, "sky"),
            P("field", None),
            P("field", None),
            P("field", None),
            P("field"),
            P("field", "sky"),
            P("field", None, None),
        ),
        out_specs=P(("field", "epoch"), "sky"),
        check_vma=False,
    )
```

profile of v0, /device:TPU:17, one launch (start us, length us, event | category | flops | bytes accessed | tf_op | source)
XLA Modules:
  0.0 385.4 jit_solution(12242590850483263235)
XLA Ops:
  6.5 1.1 fusion.74
  7.6 3.7 collective-permute-start
  11.3 1.9 collective-permute-start.1
  13.2 4.3 %collective-permute-done.1 = bf16[512,16]{1,0:T(8,128)(2,1)S(1)} collective-permute-done((bf16[512,16]{1,0:T(8,128)(2,1)S(1)}, bf16[512,16]{1,0:T(8,128)(2,1)S(1)}, u32[]{:S(2)}, u32[]{:S(2)}) %collective-permute-start.1) | collective-permute-done | bytes 16416 | tf_op jit(solution)/shard_map/ppermute | solution.py:18
  17.6 2.2 pad_maximum_fusion
  19.9 53.3 %all-gather.2.cloned.1.call-done = bf16[2048,544]{1,0:T(8,128)(2,1)} async-done(((bf16[512,544]{1,0:T(8,128)(2,1)}), bf16[2048,544]{1,0:T(8,128)(2,1)}) %all-gather.2.cloned.1.call-update) | async-done | bytes 2228240 | tf_op jit(solution)/shard_map/all_gather | solution.py:56
  73.2 3.5 pad.24
  76.7 2.5 broadcast_in_dim.819
  79.2 197.8 %while.24 = (s32[]{:T(128)}, f32[2080,544]{0,1:T(8,128)}, s32[]{:T(128)}, s32[8,4,4]{0,2,1:T(4,128)}, s32[]{:T(128)}, /*index=5*/s32[8,2]{0,1:T(2,128)S(1)}, bf1...) while((s32[]{:T(128)}, f32[2080,544]{0,1:T(8,128)}, ...), condition=%wide.region_9.10_spmd, body=%wide.region_0.9_spmd.sunk | while | flops 4757068288 | bytes 58701516 | solution.py:96
  97.8 3.5 add_convert_fusion.5
  101.3 0.7 fusion.100
  118.5 3.5 add_convert_fusion.4
  122.0 1.6 constant_dynamic-slice_fusion.13
  124.8 0.7 dynamic-slice_convert_fusion.2
  125.5 3.1 constant_dynamic-slice_fusion.16
  129.2 4.3 %conditional.8 = (f32[544,544]{0,1:T(8,128)S(1)}) conditional(s32[]{:T(128)} %convert_element_type.900, () %tuple.186, (s32[]{:T(128)}, f32[]{:T(128)}, f32[512]{0:T(512)S(1)}, bf16[2080,544]{1,0:T(8,128)(2,1)}, bf16[544,512]{1,0:T(8,128)(2,1)S(1)}, /*index=5*/bf16[544,512]{1,0:T(8,128)(2,1)S(1)}, bf16[1,2048,512]{2,1,0:T(8,128)(2,1)}) %tuple.212), branch_computations={%region_1.1_spmd, %region_2.2_spmd} | conditional | flops 1178108416 | bytes 5687328 | solution.py:90
  129.8 2.4 fusion.1
  132.2 1.3 convolution_bitcast_fusion
  133.5 1.5 slice_add_fusion.8
  135.0 8.0 %scatter-add.40 = f32[2080,544]{0,1:T(8,128)} dynamic-update-slice(f32[2080,544]{0,1:T(8,128)} %get-tuple-element.1017, f32[544,544]{0,1:T(8,128)S(1)} %slice_add_fusion.8, s32[]{:T(128)} %constant.688.clone.1..sunk, s32[]{:T(128)} %constant.688.clone.1..sunk) | dynamic-update-slice | bytes 2367492 | tf_op jit(solution)/shard_map/while/body/eval_jaxpr/scatter-add | solution.py:91
  143.6 4.7 %conditional.9 = (f32[544,544]{0,1:T(8,128)S(1)}) conditional(s32[]{:T(128)} %convert_element_type.901, () %tuple.188, (s32[]{:T(128)}, f32[]{:T(128)}, f32[512]{0:T(512)S(1)}, bf16[2080,544]{1,0:T(8,128)(2,1)}, bf16[544,512]{1,0:T(8,128)(2,1)}, /*index=5*/bf16[544,512]{1,0:T(8,128)(2,1)S(1)}, bf16[1,2048,512]{2,1,0:T(8,128)(2,1)}) %tuple.213), branch_computations={%region_3.3_spmd, %region_4.4_spmd} | conditional | flops 1178108416 | bytes 7915580 | solution.py:90
  144.3 2.7 fusion.5
  147.0 1.3 convolution_bitcast_fusion.1
  148.3 1.5 slice_add_fusion.9
  149.8 7.9 %scatter-add.41 = f32[2080,544]{0,1:T(8,128)} dynamic-update-slice(f32[2080,544]{0,1:T(8,128)} %scatter-add.40, f32[544,544]{0,1:T(8,128)S(1)} %slice_add_fusion.9, s32[]{:T(128)} %constant.694.clone.1..sunk, s32[]{:T(128)} %constant.688.clone.1..sunk) | dynamic-update-slice | bytes 2367492 | tf_op jit(solution)/shard_map/while/body/eval_jaxpr/scatter-add | solution.py:91
  158.4 4.7 %conditional.10 = (f32[544,544]{0,1:T(8,128)S(1)}) conditional(s32[]{:T(128)} %convert_element_type.902, () %tuple.190, (s32[]{:T(128)}, f32[]{:T(128)}, f32[512]{0:T(512)S(1)}, bf16[2080,544]{1,0:T(8,128)(2,1)}, bf16[544,512]{1,0:T(8,128)(2,1)}, /*index=5*/bf16[544,512]{1,0:T(8,128)(2,1)S(1)}, bf16[1,2048,512]{2,1,0:T(8,128)(2,1)}) %tuple.214), branch_computations={%region_5.5_spmd, %region_6.6_spmd} | conditional | flops 1178108416 | bytes 7915580 | solution.py:90
  159.1 2.7 fusion.9
  161.8 1.3 convolution_bitcast_fusion.2
  163.1 1.5 slice_add_fusion.10
  164.6 7.8 %scatter-add.42 = f32[2080,544]{0,1:T(8,128)} dynamic-update-slice(f32[2080,544]{0,1:T(8,128)} %scatter-add.41, f32[544,544]{0,1:T(8,128)S(1)} %slice_add_fusion.10, s32[]{:T(128)} %constant.685.clone.1..sunk, s32[]{:T(128)} %constant.688.clone.1..sunk) | dynamic-update-slice | bytes 2367492 | tf_op jit(solution)/shard_map/while/body/eval_jaxpr/scatter-add | solution.py:91
  172.9 4.6 %conditional.11 = (f32[544,544]{0,1:T(8,128)S(1)}) conditional(s32[]{:T(128)} %convert_element_type.903, () %tuple.192, (s32[]{:T(128)}, f32[]{:T(128)}, f32[512]{0:T(512)S(1)}, bf16[2080,544]{1,0:T(8,128)(2,1)}, bf16[544,512]{1,0:T(8,128)(2,1)}, /*index=5*/bf16[544,512]{1,0:T(8,128)(2,1)S(1)}, bf16[1,2048,512]{2,1,0:T(8,128)(2,1)}) %tuple.215), branch_computations={%region_7.7_spmd, %region_8.8_spmd} | conditional | flops 1178108416 | bytes 7915580 | solution.py:90
  173.5 2.7 fusion.13
  176.2 1.3 convolution_bitcast_fusion.3
  177.5 2.7 fusion.104
  198.8 3.5 add_convert_fusion.5
  202.3 0.7 fusion.100
  219.5 3.5 add_convert_fusion.4
  223.0 1.6 constant_dynamic-slice_fusion.13
  226.5 3.1 constant_dynamic-slice_fusion.16
  230.3 1.5 slice_add_fusion.8
  231.8 8.0 %scatter-add.40 = f32[2080,544]{0,1:T(8,128)} dynamic-update-slice(f32[2080,544]{0,1:T(8,128)} %get-tuple-element.1017, f32[544,544]{0,1:T(8,128)S(1)} %slice_add_fusion.8, s32[]{:T(128)} %constant.688.clone.1..sunk, s32[]{:T(128)} %constant.688.clone.1..sunk) | dynamic-update-slice | bytes 2367492 | tf_op jit(solution)/shard_map/while/body/eval_jaxpr/scatter-add | solution.py:91
  240.4 4.7 %conditional.9 = (f32[544,544]{0,1:T(8,128)S(1)}) conditional(s32[]{:T(128)} %convert_element_type.901, () %tuple.188, (s32[]{:T(128)}, f32[]{:T(128)}, f32[512]{0:T(512)S(1)}, bf16[2080,544]{1,0:T(8,128)(2,1)}, bf16[544,512]{1,0:T(8,128)(2,1)}, /*index=5*/bf16[544,512]{1,0:T(8,128)(2,1)S(1)}, bf16[1,2048,512]{2,1,0:T(8,128)(2,1)}) %tuple.213), branch_computations={%region_3.3_spmd, %region_4.4_spmd} | conditional | flops 1178108416 | bytes 7915580 | solution.py:90
  241.1 2.7 fusion.5
  243.8 1.3 convolution_bitcast_fusion.1
  245.1 1.5 slice_add_fusion.9
  246.6 7.9 %scatter-add.41 = f32[2080,544]{0,1:T(8,128)} dynamic-update-slice(f32[2080,544]{0,1:T(8,128)} %scatter-add.40, f32[544,544]{0,1:T(8,128)S(1)} %slice_add_fusion.9, s32[]{:T(128)} %constant.694.clone.1..sunk, s32[]{:T(128)} %constant.688.clone.1..sunk) | dynamic-update-slice | bytes 2367492 | tf_op jit(solution)/shard_map/while/body/eval_jaxpr/scatter-add | solution.py:91
  255.2 4.7 %conditional.10 = (f32[544,544]{0,1:T(8,128)S(1)}) conditional(s32[]{:T(128)} %convert_element_type.902, () %tuple.190, (s32[]{:T(128)}, f32[]{:T(128)}, f32[512]{0:T(512)S(1)}, bf16[2080,544]{1,0:T(8,128)(2,1)}, bf16[544,512]{1,0:T(8,128)(2,1)}, /*index=5*/bf16[544,512]{1,0:T(8,128)(2,1)S(1)}, bf16[1,2048,512]{2,1,0:T(8,128)(2,1)}) %tuple.214), branch_computations={%region_5.5_spmd, %region_6.6_spmd} | conditional | flops 1178108416 | bytes 7915580 | solution.py:90
  255.9 2.7 fusion.9
  258.6 1.3 convolution_bitcast_fusion.2
  259.9 1.5 slice_add_fusion.10
  261.4 7.8 %scatter-add.42 = f32[2080,544]{0,1:T(8,128)} dynamic-update-slice(f32[2080,544]{0,1:T(8,128)} %scatter-add.41, f32[544,544]{0,1:T(8,128)S(1)} %slice_add_fusion.10, s32[]{:T(128)} %constant.685.clone.1..sunk, s32[]{:T(128)} %constant.688.clone.1..sunk) | dynamic-update-slice | bytes 2367492 | tf_op jit(solution)/shard_map/while/body/eval_jaxpr/scatter-add | solution.py:91
  269.7 4.6 %conditional.11 = (f32[544,544]{0,1:T(8,128)S(1)}) conditional(s32[]{:T(128)} %convert_element_type.903, () %tuple.192, (s32[]{:T(128)}, f32[]{:T(128)}, f32[512]{0:T(512)S(1)}, bf16[2080,544]{1,0:T(8,128)(2,1)}, bf16[544,512]{1,0:T(8,128)(2,1)}, /*index=5*/bf16[544,512]{1,0:T(8,128)(2,1)S(1)}, bf16[1,2048,512]{2,1,0:T(8,128)(2,1)}) %tuple.215), branch_computations={%region_7.7_spmd, %region_8.8_spmd} | conditional | flops 1178108416 | bytes 7915580 | solution.py:90
  270.3 2.7 fusion.13
  273.0 1.3 convolution_bitcast_fusion.3
  274.3 2.7 fusion.104
  277.0 1.1 fusion.73
  278.1 3.7 collective-permute-start.2
  282.4 5.4 %slice.992 = f32[2048,512]{0,1:T(8,128)} slice(f32[2080,544]{0,1:T(8,128)} %get-tuple-element.722), slice={[16:2064], [16:528]} | slice | bytes 8388608 | tf_op jit(solution)/shard_map/slice | solution.py:104
  287.8 1.9 collective-permute-start.3
  289.7 2.3 fusion.67
  292.1 2.0 collective-permute-done.3
  294.1 1.6 fusion.68
  295.7 80.3 %reduce-scatter.2.cloned.1.call-done = f32[512,512]{0,1:T(8,128)} async-done(((f32[2048,512]{0,1:T(8,128)}), f32[512,512]{0,1:T(8,128)}) %reduce-scatter.2.cloned.1.call-update) | async-done | bytes 1048592 | tf_op jit(solution)/shard_map/reduce_scatter | solution.py:108
  376.0 2.5 copy.13
  (49 shorter events, 9.6 us)
Async XLA Ops:
  6.5 66.7 %all-gather.2.cloned.1.call-start = ((), (), s32[]{:S(2)}) async-start(), calls=%async_computation.1 | async-start | bytes 3276800 | tf_op jit(solution)/shard_map/all_gather | solution.py:56
  7.6 5.6 %collective-permute-start = (bf16[512,16]{1,0:T(8,128)(2,1)S(1)}, bf16[512,16]{1,0:T(8,128)(2,1)S(1)}, u32[]{:S(2)}, u32[]{:S(2)}) collective-permute-start(bf16[512,16]{1,0:T(8,128)(2,1)S(1)} %get-tuple-element.807), channel_id=1, source_target_pairs={{0,1},{1,2},{2,3},{4,5},{5,6},{6,7},{8,9},{9,10},{10,11},{12,13},{... | collective-permute-start | bytes 49160 | tf_op jit(solution)/shard_map/ppermute | solution.py:17
  11.3 6.3 %collective-permute-start.1 = (bf16[512,16]{1,0:T(8,128)(2,1)S(1)}, bf16[512,16]{1,0:T(8,128)(2,1)S(1)}, u32[]{:S(2)}, u32[]{:S(2)}) collective-permute-start(bf16[512,16]{1,0:T(8,128)(2,1)S(1)} %get-tuple-element.808), channel_id=1, source_target_pairs={{1,0},{2,1},{3,2},{5,4},{6,5},{7,6},{9,8},{10,9},{11,10},{13,12},{... | collective-permute-start | bytes 49160 | tf_op jit(solution)/shard_map/ppermute | solution.py:18
  19.9 356.1 %reduce-scatter.2.cloned.1.call-start = ((), (), s32[]{:S(2)}) async-start(), calls=%async_computation.2 | async-start | bytes 5242880 | tf_op jit(solution)/shard_map/reduce_scatter | solution.py:108
  76.7 2.5 copy-start.4
  76.7 2.5 copy-start.5
  122.0 7.2 %copy-start = (bf16[544,512]{1,0:T(8,128)(2,1)}, bf16[544,512]{1,0:T(8,128)(2,1)S(1)}, u32[]{:S(2)}) copy-start(bf16[544,512]{1,0:T(8,128)(2,1)S(1)} %add_convert_fusion.4) | copy-start | bytes 1671172 | tf_op jit(solution)/shard_map/while
  144.3 2.7 copy-start.1
  159.1 2.7 copy-start.2
  173.5 2.7 copy-start.3
  223.0 7.2 %copy-start = (bf16[544,512]{1,0:T(8,128)(2,1)}, bf16[544,512]{1,0:T(8,128)(2,1)S(1)}, u32[]{:S(2)}) copy-start(bf16[544,512]{1,0:T(8,128)(2,1)S(1)} %add_convert_fusion.4) | copy-start | bytes 1671172 | tf_op jit(solution)/shard_map/while
  241.1 2.7 copy-start.1
  255.9 2.7 copy-start.2
  270.3 2.7 copy-start.3
  278.1 11.6 %collective-permute-start.2 = (f32[2048,16]{0,1:T(8,128)S(1)}, f32[2048,16]{0,1:T(8,128)S(1)}, u32[]{:S(2)}, u32[]{:S(2)}) collective-permute-start(f32[2048,16]{0,1:T(8,128)S(1)} %get-tuple-element.806), channel_id=1, source_target_pairs={{0,1},{1,2},{2,3},{4,5},{5,6},{6,7},{8,9},{9,10},{10,11},{12,13},{... | collective-permute-start | bytes 393224 | tf_op jit(solution)/shard_map/ppermute | solution.py:17
  287.8 6.3 %collective-permute-start.3 = (f32[2048,16]{0,1:T(8,128)S(1)}, f32[2048,16]{0,1:T(8,128)S(1)}, u32[]{:S(2)}, u32[]{:S(2)}) collective-permute-start(f32[2048,16]{0,1:T(8,128)S(1)} %get-tuple-element.805), channel_id=1, source_target_pairs={{1,0},{2,1},{3,2},{5,4},{6,5},{7,6},{9,8},{10,9},{11,10},{13,12},{... | collective-permute-start | bytes 393224 | tf_op jit(solution)/shard_map/ppermute | solution.py:18
Sparse Core Ops, SparseCore 0:
  20.0 53.2 all-gather.1
  295.8 80.1 reduce-scatter.1
where the time goes:
time: 390 us; the launch traced here: 385 us
  waiting for transfers between devices  140 us (36%)
  local copies, waits for them, and re-layouts  82.3 us (21%)
  loops' own time  74.2 us (19%)
  other arithmetic  36.6 us (9%)
  matrix products  27.5 us (7%)
  between operations  13.5 us (3%)
  starting transfers between devices  11.2 us (3%)
    reduce_scatter x1, waiting for transfers between devices, strip_plan(): lax.psum_scatter(center_cells, 'epoch', scatter_dimension=0, tiled=True)  80.3 us
    another operation x1, loops' own time, strip_plan(): lax.fori_loop(0, local_count, per_epoch, jnp.zeros((full_rows + 2 * HALO,...  69.6 us
    all_gather x1, waiting for transfers between devices, strip_plan(): strip_cells = lax.all_gather(slab_cells, 'epoch', axis=0, tiled=True)  53.3 us
    scatter-add x6, local copies, waits for them, and re-layouts, per_epoch(): running.at[row_block * TILE:row_block * TILE + TILE + 2 * HALO]  47.3 us
    dot_general x7, matrix products, epoch_block(): modeled = jnp.dot(lifted, col_table, preferred_element_type=jnp.float32)  18.5 us
    convert_element_type x4, other arithmetic, band_tables(): return band_table.astype(jnp.bfloat16)  14.1 us
    dot_general x7, matrix products, epoch_block(): return jnp.dot(row_table, pulled, preferred_element_type=jnp.float32)  9.02 us
    add x6, other arithmetic, per_epoch(): running.at[row_block * TILE:row_block * TILE + TILE + 2 * HALO]  8.95 us
  transfers between devices with their start and end apart: 6, of which 4 were waited for; matrix products, arithmetic and copies ran while one was open for 2% of the time, Pallas kernels for 0%

commit v1 on v0

--- a/solution.py
+++ b/solution.py
@@ -1,10 +1,22 @@
+import functools
 import jax
 import jax.numpy as jnp
 from jax import lax
+from jax.experimental import pallas as pl
+from jax.experimental.pallas import tpu as pltpu
 from jax.sharding import PartitionSpec as P
 
 TILE = 512
 HALO = 16
+MESH = pl.DeviceIdType.MESH
+ROWS = 512
+COLS = 512
+PAD = 128
+WIDE = COLS + 2 * PAD
+SUB = 128
+REACH = SUB + 2 * HALO
+CHUNK = 256
+PARTS = ROWS // CHUNK
 
 
 def extended(value, sides, width):
@@ -108,10 +120,450 @@
     return lax.psum_scatter(center_cells, "epoch", scatter_dimension=0, tiled=True)
 
 
-def on_device(sky_scene, images, psf_rows, psf_cols, offsets, epoch_weight, column_mask, coverage):
-    return strip_plan(
-        sky_scene, images, psf_rows, psf_cols, offsets, epoch_weight, column_mask, coverage
+def band(position, psf_ref, epoch, first, taps):
+    table = jnp.zeros(position.shape, jnp.float32)
+    for tap in range(taps):
+        table = jnp.where(position == tap, psf_ref[epoch, first + tap], table)
+    return table.astype(jnp.bfloat16)
+
+
+def fused_kernel(
+    n, sky_count, taps, local,
+    psf_ref, offset_ref, factor_ref, mask_ref, scene_ref, image_ref, out_ref,
+    strip, acc, image_buf, row_tab, rowt_tab, col_tab, lift, res, pull,
+    edge_out, edge_in, send_r, recv_r, send_l, recv_l,
+    load_sem, image_sem,
+    ag_r_send, ag_r_recv, ag_l_send, ag_l_recv,
+    sky_r_send, sky_r_recv, sky_l_send, sky_l_recv,
+    rs_r_send, rs_r_recv, rs_l_send, rs_l_recv,
+    ed_r_send, ed_r_recv, ed_l_send, ed_l_recv,
+):
+    me = lax.axis_index("epoch")
+    sky = lax.axis_index("sky")
+    total = n * ROWS
+    has_up, has_down = me > 0, me < n - 1
+    has_left, has_right = sky > 0, sky < sky_count - 1
+    base = me * local
+    half = (taps - 1) // 2
+
+    def rows_of(block, part=None):
+        if part is None:
+            return pl.ds(pl.multiple_of(HALO + block * ROWS, HALO), ROWS)
+        return pl.ds(pl.multiple_of(HALO + block * ROWS + part * CHUNK, HALO), CHUNK)
+
+    centre = pl.ds(PAD, COLS)
+    load = pltpu.make_async_copy(scene_ref, strip.at[rows_of(me), centre], load_sem)
+    load.start()
+    image_loads = [
+        pltpu.make_async_copy(image_ref.at[e], image_buf.at[e], image_sem.at[e])
+        for e in range(local)
+    ]
+
+    barrier = pltpu.get_barrier_semaphore()
+    greetings = (
+        (has_up, {"epoch": me - 1}),
+        (has_down, {"epoch": me + 1}),
+        (has_left, {"sky": sky - 1}),
+        (has_right, {"sky": sky + 1}),
     )
+    for there, where in greetings:
+        @pl.when(there)
+        def _():
+            pl.semaphore_signal(barrier, inc=1, device_id=where, device_id_type=MESH)
+    pl.semaphore_wait(barrier, sum(there.astype(jnp.int32) for there, where in greetings))
+
+    def remote(src, dst, ssem, rsem, where):
+        return pltpu.make_async_remote_copy(
+            src_ref=src, dst_ref=dst, send_sem=ssem, recv_sem=rsem,
+            device_id=where, device_id_type=MESH,
+        )
+
+    def gather_down(t, part):
+        piece = strip.at[rows_of(me - t, part), centre]
+        return remote(piece, piece, ag_r_send.at[t, part], ag_r_recv.at[t, part], {"epoch": me + 1})
+
+    def gather_down_in(t, part):
+        piece = strip.at[rows_of(me - 1 - t, part), centre]
+        return remote(piece, piece, ag_r_send.at[t, part], ag_r_recv.at[t, part], {"epoch": me - 1})
+
+    def gather_up(t, part):
+        piece = strip.at[rows_of(me + t, part), centre]
+        return remote(piece, piece, ag_l_send.at[t, part], ag_l_recv.at[t, part], {"epoch": me - 1})
+
+    def gather_up_in(t, part):
+        piece = strip.at[rows_of(me + 1 + t, part), centre]
+        return remote(piece, piece, ag_l_send.at[t, part], ag_l_recv.at[t, part], {"epoch": me + 1})
+
+    def sky_right(block):
+        return remote(
+            strip.at[rows_of(block), pl.ds(COLS, PAD)], strip.at[rows_of(block), pl.ds(0, PAD)],
+            sky_r_send.at[block], sky_r_recv.at[block], {"sky": sky + 1},
+        )
+
+    def sky_right_in(block):
+        return remote(
+            strip.at[rows_of(block), pl.ds(COLS, PAD)], strip.at[rows_of(block), pl.ds(0, PAD)],
+            sky_r_send.at[block], sky_r_recv.at[block], {"sky": sky - 1},
+        )
+
+    def sky_left(block):
+        return remote(
+            strip.at[rows_of(block), pl.ds(PAD, PAD)], strip.at[rows_of(block), pl.ds(PAD + COLS, PAD)],
+            sky_l_send.at[block], sky_l_recv.at[block], {"sky": sky - 1},
+        )
+
+    def sky_left_in(block):
+        return remote(
+            strip.at[rows_of(block), pl.ds(PAD, PAD)], strip.at[rows_of(block), pl.ds(PAD + COLS, PAD)],
+            sky_l_send.at[block], sky_l_recv.at[block], {"sky": sky + 1},
+        )
+
+    def send_edges(block):
+        @pl.when(has_right)
+        def _():
+            sky_right(block).start()
+
+        @pl.when(has_left)
+        def _():
+            sky_left(block).start()
+
+    def wait_edges(block):
+        @pl.when(has_left)
+        def _():
+            sky_right_in(block).wait_recv()
+
+        @pl.when(has_right)
+        def _():
+            sky_left_in(block).wait_recv()
+
+    load.wait()
+    for part in range(PARTS):
+        @pl.when(has_down)
+        def _():
+            gather_down(0, part).start()
+
+        @pl.when(has_up)
+        def _():
+            gather_up(0, part).start()
+    send_edges(me)
+    for copy in image_loads:
+        copy.start()
+
+    strip[pl.ds(0, HALO), :] = jnp.zeros((HALO, WIDE), jnp.bfloat16)
+    strip[pl.ds(HALO + total, HALO), :] = jnp.zeros((HALO, WIDE), jnp.bfloat16)
+
+    @pl.when(sky == 0)
+    def _():
+        strip[pl.ds(HALO, total), pl.ds(0, PAD)] = jnp.zeros((total, PAD), jnp.bfloat16)
+
+    @pl.when(sky == sky_count - 1)
+    def _():
+        strip[pl.ds(HALO, total), pl.ds(PAD + COLS, PAD)] = jnp.zeros((total, PAD), jnp.bfloat16)
+
+    def clear(i, carry):
+        acc[pl.ds(pl.multiple_of(i * 32, 32), 32), :] = jnp.zeros((32, WIDE), jnp.float32)
+        return carry
+
+    lax.fori_loop(0, (total + 2 * HALO) // 32, clear, 0)
+
+    for e in range(local):
+        shift_r = offset_ref[base + e, 0]
+        shift_c = offset_ref[base + e, 1]
+        out_i = lax.broadcasted_iota(jnp.int32, (SUB, REACH), 0)
+        in_i = lax.broadcasted_iota(jnp.int32, (SUB, REACH), 1)
+        row_tab[e] = band(in_i - out_i - HALO - shift_r + half, psf_ref, base + e, 0, taps)
+        in_t = lax.broadcasted_iota(jnp.int32, (REACH, SUB), 0)
+        out_t = lax.broadcasted_iota(jnp.int32, (REACH, SUB), 1)
+        rowt_tab[:, e * SUB : (e + 1) * SUB] = band(
+            in_t - out_t - HALO - shift_r + half, psf_ref, base + e, 0, taps
+        )
+
+        def fill(i, carry):
+            k = lax.broadcasted_iota(jnp.int32, (64, 256), 0) + i * 64
+            j = lax.broadcasted_iota(jnp.int32, (64, 256), 1)
+            col_tab[e, pl.ds(pl.multiple_of(i * 64, 64), 64), :] = band(
+                k - j - PAD - shift_c + half, psf_ref, base + e, taps, taps
+            )
+            return carry
+
+        lax.fori_loop(0, 8, fill, 0)
+
+    def compute(q, carry):
+        r0 = pl.multiple_of(q * CHUNK, CHUNK)
+        for e in range(local):
+            for u in range(2):
+                window = strip[pl.ds(pl.multiple_of(r0 + u * SUB, SUB), REACH), :]
+                lift[u * SUB : (u + 1) * SUB, :] = jnp.dot(
+                    row_tab[e], window, preferred_element_type=jnp.float32
+                ).astype(jnp.bfloat16)
+            factor = factor_ref[base + e, q // PARTS] * mask_ref[pl.ds(base + e, 1), :].astype(
+                jnp.float32
+            )
+            for h in range(2):
+                cols = slice(h * 256, (h + 1) * 256)
+                modeled = jnp.dot(
+                    lift[:, h * 256 : h * 256 + 512], col_tab[e], preferred_element_type=jnp.float32
+                )
+                seen = image_buf[e, pl.ds(r0, CHUNK), cols].astype(jnp.float32)
+                res[:, cols] = (factor[:, cols] * (modeled - seen)).astype(jnp.bfloat16)
+
+            def back(h, side):
+                return lax.dot_general(
+                    res[:, h * 256 : (h + 1) * 256],
+                    col_tab[e, side * 256 : (side + 1) * 256, :],
+                    (((1,), (1,)), ((), ())),
+                    preferred_element_type=jnp.float32,
+                )
+
+            pulls = (back(0, 0), back(0, 1) + back(1, 0), back(1, 1))
+            for third, value in enumerate(pulls):
+                narrow = value.astype(jnp.bfloat16)
+                for u in range(2):
+                    pull[u, e * SUB : (e + 1) * SUB, third * 256 : (third + 1) * 256] = narrow[
+                        u * SUB : (u + 1) * SUB
+                    ]
+        for u in range(2):
+            where = pl.ds(pl.multiple_of(r0 + u * SUB, SUB), REACH)
+            acc[where, :] += jnp.dot(rowt_tab[...], pull[u], preferred_element_type=jnp.float32)
+        return carry
+
+    for copy in image_loads:
+        copy.wait()
+    wait_edges(me)
+
+    def ready(t):
+        low = jnp.maximum(me - t, 0)
+        high = jnp.minimum(me + t, n - 1)
+        first = jnp.where(low == 0, 0, low + 1)
+        stop = jnp.where(high == n - 1, n, high)
+        return first, jnp.maximum(stop, first)
+
+    for t in range(n - 1):
+        for part in range(PARTS):
+            @pl.when(me - 1 - t >= 0)
+            def _():
+                gather_down_in(t, part).wait_recv()
+                if t + 1 < n - 1:
+                    @pl.when(has_down)
+                    def _():
+                        gather_down(t + 1, part).start()
+
+            @pl.when(me + 1 + t <= n - 1)
+            def _():
+                gather_up_in(t, part).wait_recv()
+                if t + 1 < n - 1:
+                    @pl.when(has_up)
+                    def _():
+                        gather_up(t + 1, part).start()
+
+        @pl.when(me - 1 - t >= 0)
+        def _():
+            send_edges(me - 1 - t)
+
+        @pl.when(me + 1 + t <= n - 1)
+        def _():
+            send_edges(me + 1 + t)
+
+        @pl.when(me - 1 - t >= 0)
+        def _():
+            wait_edges(me - 1 - t)
+
+        @pl.when(me + 1 + t <= n - 1)
+        def _():
+            wait_edges(me + 1 + t)
+
+        first, stop = ready(t + 1)
+        if t == 0:
+            lax.fori_loop(first * PARTS, stop * PARTS, compute, 0)
+        else:
+            done_first, done_stop = ready(t)
+            empty = done_stop <= done_first
+            below_stop = jnp.where(empty, stop, done_first)
+            above_first = jnp.where(empty, stop, done_stop)
+            lax.fori_loop(first * PARTS, below_stop * PARTS, compute, 0)
+            lax.fori_loop(above_first * PARTS, stop * PARTS, compute, 0)
+
+    def grad_right(block, where):
+        return remote(edge_out.at[1, block], edge_in.at[0, block], ed_r_send.at[block], ed_r_recv.at[block], where)
+
+    def grad_left(block, where):
+        return remote(edge_out.at[0, block], edge_in.at[1, block], ed_l_send.at[block], ed_l_recv.at[block], where)
+
+    order = []
+    for k in range(n):
+        for block in (n - 1 - k, k):
+            if block not in order:
+                order.append(block)
+    for block in order:
+        rows = pl.ds(HALO + block * ROWS, ROWS)
+        edge_out[0, block] = acc[rows, 0:PAD].astype(jnp.bfloat16)
+        edge_out[1, block] = acc[rows, PAD + COLS : WIDE].astype(jnp.bfloat16)
+
+        @pl.when(has_right)
+        def _():
+            grad_right(block, {"sky": sky + 1}).start()
+
+        @pl.when(has_left)
+        def _():
+            grad_left(block, {"sky": sky - 1}).start()
+
+    def merge_edges(block):
+        rows = pl.ds(HALO + block * ROWS, ROWS)
+
+        @pl.when(has_left)
+        def _():
+            grad_right(block, {"sky": sky - 1}).wait_recv()
+            acc[rows, PAD : 2 * PAD] += edge_in[0, block].astype(jnp.float32)
+
+        @pl.when(has_right)
+        def _():
+            grad_left(block, {"sky": sky + 1}).wait_recv()
+            acc[rows, COLS : COLS + PAD] += edge_in[1, block].astype(jnp.float32)
+
+    def reduce_down(block, part, where):
+        rows = pl.ds(part * CHUNK, CHUNK)
+        return remote(send_r.at[block, rows], recv_r.at[block, rows], rs_r_send.at[block, part], rs_r_recv.at[block, part], where)
+
+    def reduce_up(block, part, where):
+        rows = pl.ds(part * CHUNK, CHUNK)
+        return remote(send_l.at[block, rows], recv_l.at[block, rows], rs_l_send.at[block, part], rs_l_recv.at[block, part], where)
+
+    def pass_on(block, part, down):
+        rows = pl.ds(part * CHUNK, CHUNK)
+        mine = pl.ds(HALO + block * ROWS + part * CHUNK, CHUNK)
+        staged, arrived = (send_r, recv_r) if down else (send_l, recv_l)
+        move = reduce_down if down else reduce_up
+        fed = has_up if down else has_down
+        out_to = {"epoch": me + 1} if down else {"epoch": me - 1}
+        in_from = {"epoch": me - 1} if down else {"epoch": me + 1}
+
+        @pl.when(fed)
+        def _():
+            move(block, part, in_from).wait_recv()
+            staged[block, rows] = (
+                acc[mine, PAD : PAD + COLS] + arrived[block, rows].astype(jnp.float32)
+            ).astype(jnp.bfloat16)
+
+        @pl.when(jnp.logical_not(fed))
+        def _():
+            staged[block, rows] = acc[mine, PAD : PAD + COLS].astype(jnp.bfloat16)
+
+        move(block, part, out_to).start()
+
+    for block in order:
+        merge_edges(block)
+    for k in range(n - 1):
+        down_block, up_block = n - 1 - k, k
+        for part in range(PARTS):
+            @pl.when(me < down_block)
+            def _():
+                pass_on(down_block, part, True)
+
+            @pl.when(me > up_block)
+            def _():
+                pass_on(up_block, part, False)
+
+    for part in range(PARTS):
+        rows = pl.ds(part * CHUNK, CHUNK)
+        mine = pl.ds(pl.multiple_of(HALO + me * ROWS + part * CHUNK, HALO), CHUNK)
+        out_ref[rows, :] = acc[mine, PAD : PAD + COLS]
+
+        @pl.when(has_up)
+        def _():
+            reduce_down(me, part, {"epoch": me - 1}).wait_recv()
+            out_ref[rows, :] += recv_r[me, rows].astype(jnp.float32)
+
+        @pl.when(has_down)
+        def _():
+            reduce_up(me, part, {"epoch": me + 1}).wait_recv()
+            out_ref[rows, :] += recv_l[me, rows].astype(jnp.float32)
+
+    for t in range(n - 1):
+        for part in range(PARTS):
+            @pl.when(has_down & (me - t >= 0))
+            def _():
+                gather_down(t, part).wait_send()
+
+            @pl.when(has_up & (me + t <= n - 1))
+            def _():
+                gather_up(t, part).wait_send()
+
+            @pl.when(me < n - 1 - t)
+            def _():
+                reduce_down(n - 1 - t, part, {"epoch": me + 1}).wait_send()
+
+            @pl.when(me > t)
+            def _():
+                reduce_up(t, part, {"epoch": me - 1}).wait_send()
+    for block in range(n):
+        @pl.when(has_right)
+        def _():
+            sky_right(block).wait_send()
+            grad_right(block, {"sky": sky + 1}).wait_send()
+
+        @pl.when(has_left)
+        def _():
+            sky_left(block).wait_send()
+            grad_left(block, {"sky": sky - 1}).wait_send()
+
+
+def fused_plan(sky_scene, images, psf_rows, psf_cols, offsets, epoch_weight, column_mask, coverage):
+    n, sky_count = lax.axis_size("epoch"), lax.axis_size("sky")
+    local, total = images.shape[0], images.shape[1]
+    taps = psf_rows.shape[1]
+    psf = jnp.concatenate([psf_rows, psf_cols], axis=1).astype(jnp.float32)
+    tile_column = lax.axis_index("sky") * COLS // TILE
+    tiles = lax.dynamic_index_in_dim(coverage, tile_column, 2, keepdims=False)
+    factor = 2.0 * epoch_weight[:, None] * tiles.astype(jnp.float32)
+    bf, f32 = jnp.bfloat16, jnp.float32
+    smem = pl.BlockSpec(memory_space=pltpu.SMEM)
+    vmem = pl.BlockSpec(memory_space=pltpu.VMEM)
+    anywhere = pl.BlockSpec(memory_space=pl.ANY)
+    dma = pltpu.SemaphoreType.DMA
+    return pl.pallas_call(
+        functools.partial(fused_kernel, n, sky_count, taps, local),
+        out_shape=jax.ShapeDtypeStruct((ROWS, COLS), f32),
+        in_specs=[smem, smem, smem, vmem, anywhere, anywhere],
+        out_specs=vmem,
+        scratch_shapes=[
+            pltpu.VMEM((total + 2 * HALO, WIDE), bf),
+            pltpu.VMEM((total + 2 * HALO, WIDE), f32),
+            pltpu.VMEM((local, total, COLS), bf),
+            pltpu.VMEM((local, SUB, REACH), bf),
+            pltpu.VMEM((REACH, local * SUB), bf),
+            pltpu.VMEM((local, 512, 256), bf),
+            pltpu.VMEM((CHUNK, WIDE), bf),
+            pltpu.VMEM((CHUNK, COLS), bf),
+            pltpu.VMEM((2, local * SUB, WIDE), bf),
+            pltpu.VMEM((2, n, ROWS, PAD), bf),
+            pltpu.VMEM((2, n, ROWS, PAD), bf),
+            pltpu.VMEM((n, ROWS, COLS), bf),
+            pltpu.VMEM((n, ROWS, COLS), bf),
+            pltpu.VMEM((n, ROWS, COLS), bf),
+            pltpu.VMEM((n, ROWS, COLS), bf),
+            dma,
+            dma((local,)),
+        ]
+        + [dma((n, PARTS))] * 4
+        + [dma((n,))] * 4
+        + [dma((n, PARTS))] * 4
+        + [dma((n,))] * 4,
+        compiler_params=pltpu.CompilerParams(
+            collective_id=0, has_side_effects=True, vmem_limit_bytes=48 << 20
+        ),
+    )(psf, offsets, factor, column_mask, sky_scene, images)
+
+
+def on_device(sky_scene, images, *rest):
+    n = lax.axis_size("epoch")
+    fits = (
+        2 <= n <= 4
+        and sky_scene.shape == (ROWS, COLS)
+        and images.shape[1:] == (n * ROWS, COLS)
+        and images.shape[0] <= 2
+    )
+    plan = fused_plan if fits else strip_plan
+    return plan(sky_scene, images, *rest)
 
 
 def solution(mesh):

time: 390 us -> 109 us (0.28)
  the two profiles are of different devices: /device:TPU:17 before, /device:TPU:18 now
where the time goes in v1:
time: 109 us
  Pallas kernels  101 us (93%)
  local copies, waits for them, and re-layouts  5.75 us (5%)
  other arithmetic  2.2 us (2%)
    pallas_call x1, Pallas kernels, fused_plan(): pl.pallas_call(functools.partial(fused_kernel, n, sky_count, taps, local)...  101 us
    unnamed x8, local copies, waits for them, and re-layouts  5.67 us

profile of v1, /device:TPU:18, one launch (start us, length us, event | category | flops | bytes accessed | tf_op | source)
XLA Modules:
  0.0 108.9 jit_solution(10514927996652369037)
XLA Ops:
  0.0 0.7 broadcast_multiply_fusion.1
  0.7 0.7 dynamic-slice_convert_fusion
  1.4 0.1 copy.9
  1.4 0.1 broadcast_multiply_fusion.factor_ref
  1.5 0.8 maximum_convert_fusion.psf_ref
  2.3 0.8 copy.10.offset_ref
  3.0 0.0 copy-start
  3.0 2.2 %copy-done = bf16[2,2048,512]{2,1,0:T(8,128)(2,1)S(1)} copy-done((bf16[2,2048,512]{2,1,0:T(8,128)(2,1)S(1)}, bf16[2,2048,512]{2,1,0:T(8,128)(2,1)}, u32[]{:S(2)}) %copy-start) | copy-done | bytes 4194328
  5.2 0.0 copy-start.1
  5.2 1.0 copy-done.1
  6.3 0.0 copy-start.2
  6.3 0.7 copy-done.2
  7.0 101.0 %shard_map.82 = f32[512,512]{1,0:T(8,128)S(1)} custom-call(f32[8,50]{1,0:T(8,128)S(1)} %maximum_convert_fusion.psf_ref, s32[8,2]{1,0:T(8,128)S(1)} %copy.10.offset_ref, f32[8,4]{1,0:T(8,128)S(1)} %broadcast_multiply_fusion.factor_ref, s32[8,512]{1,0:T(8,128)S(1)} %copy-done.2, bf16[512,512]{1,0:T(8,128)(2,1)S(1)} %copy-done.1, bf16[2,2048,512]{2,1,0:T(8,128)(2,1)S(1)} %copy-done), custom_call_target="tpu_custom_call" | custom-call | tf_op jit(solution)/shard_map/pallas_call | solution.py:523
  108.0 1.0 copy.12
Async XLA Ops:
  3.0 2.2 %copy-start = (bf16[2,2048,512]{2,1,0:T(8,128)(2,1)S(1)}, bf16[2,2048,512]{2,1,0:T(8,128)(2,1)}, u32[]{:S(2)}) copy-start(bf16[2,2048,512]{2,1,0:T(8,128)(2,1)} %image_ref.1) | copy-start | bytes 12582916
  5.2 1.0 copy-start.1
  6.3 0.7 copy-start.2

commit v2 on v1

--- a/solution.py
+++ b/solution.py
@@ -331,12 +331,15 @@
         copy.wait()
     wait_edges(me)
 
+    upper = me < n // 2
+    near_low = jnp.where(upper, 0, n // 2)
+
     def ready(t):
         low = jnp.maximum(me - t, 0)
         high = jnp.minimum(me + t, n - 1)
         first = jnp.where(low == 0, 0, low + 1)
         stop = jnp.where(high == n - 1, n, high)
-        return first, jnp.maximum(stop, first)
+        return jnp.maximum(first, near_low), jnp.minimum(stop, near_low + n // 2)
 
     for t in range(n - 1):
         for part in range(PARTS):
@@ -375,62 +378,62 @@
         first, stop = ready(t + 1)
         if t == 0:
             lax.fori_loop(first * PARTS, stop * PARTS, compute, 0)
-        else:
-            done_first, done_stop = ready(t)
-            empty = done_stop <= done_first
-            below_stop = jnp.where(empty, stop, done_first)
-            above_first = jnp.where(empty, stop, done_stop)
-            lax.fori_loop(first * PARTS, below_stop * PARTS, compute, 0)
-            lax.fori_loop(above_first * PARTS, stop * PARTS, compute, 0)
-
-    def grad_right(block, where):
-        return remote(edge_out.at[1, block], edge_in.at[0, block], ed_r_send.at[block], ed_r_recv.at[block], where)
-
-    def grad_left(block, where):
-        return remote(edge_out.at[0, block], edge_in.at[1, block], ed_l_send.at[block], ed_l_recv.at[block], where)
-
-    order = []
-    for k in range(n):
-        for block in (n - 1 - k, k):
-            if block not in order:
-                order.append(block)
-    for block in order:
-        rows = pl.ds(HALO + block * ROWS, ROWS)
-        edge_out[0, block] = acc[rows, 0:PAD].astype(jnp.bfloat16)
-        edge_out[1, block] = acc[rows, PAD + COLS : WIDE].astype(jnp.bfloat16)
-
+        elif t == 1:
+            @pl.when((me == 0) | (me == n - 1))
+            def _():
+                block = jnp.where(upper, 1, n - 2)
+                lax.fori_loop(block * PARTS, (block + 1) * PARTS, compute, 0)
+
+    pieces = n * PARTS
+    half_pieces = pieces // 2
+
+    def far(i):
+        return jnp.where(upper, pieces - 1 - i, i)
+
+    def near(j):
+        return jnp.where(upper, j, pieces - 1 - j)
+
+    def flat(q):
+        return pl.ds(pl.multiple_of(q * CHUNK, CHUNK), CHUNK)
+
+    def mine(q):
+        return pl.ds(pl.multiple_of(HALO + q * CHUNK, HALO), CHUNK)
+
+    def grad_right(q, where):
+        return remote(edge_out.at[1, flat(q)], edge_in.at[0, flat(q)], ed_r_send.at[q], ed_r_recv.at[q], where)
+
+    def grad_left(q, where):
+        return remote(edge_out.at[0, flat(q)], edge_in.at[1, flat(q)], ed_l_send.at[q], ed_l_recv.at[q], where)
+
+    def share(q):
         @pl.when(has_right)
         def _():
-            grad_right(block, {"sky": sky + 1}).start()
+            edge_out[1, flat(q), :] = acc[mine(q), PAD + COLS : WIDE].astype(jnp.bfloat16)
+            grad_right(q, {"sky": sky + 1}).start()
 
         @pl.when(has_left)
         def _():
-            grad_left(block, {"sky": sky - 1}).start()
-
-    def merge_edges(block):
-        rows = pl.ds(HALO + block * ROWS, ROWS)
-
+            edge_out[0, flat(q), :] = acc[mine(q), 0:PAD].astype(jnp.bfloat16)
+            grad_left(q, {"sky": sky - 1}).start()
+
+    def merge(q):
         @pl.when(has_left)
         def _():
-            grad_right(block, {"sky": sky - 1}).wait_recv()
-            acc[rows, PAD : 2 * PAD] += edge_in[0, block].astype(jnp.float32)
+            grad_right(q, {"sky": sky - 1}).wait_recv()
+            acc[mine(q), PAD : 2 * PAD] += edge_in[0, flat(q), :].astype(jnp.float32)
 
         @pl.when(has_right)
         def _():
-            grad_left(block, {"sky": sky + 1}).wait_recv()
-            acc[rows, COLS : COLS + PAD] += edge_in[1, block].astype(jnp.float32)
-
-    def reduce_down(block, part, where):
-        rows = pl.ds(part * CHUNK, CHUNK)
-        return remote(send_r.at[block, rows], recv_r.at[block, rows], rs_r_send.at[block, part], rs_r_recv.at[block, part], where)
-
-    def reduce_up(block, part, where):
-        rows = pl.ds(part * CHUNK, CHUNK)
-        return remote(send_l.at[block, rows], recv_l.at[block, rows], rs_l_send.at[block, part], rs_l_recv.at[block, part], where)
-
-    def pass_on(block, part, down):
-        rows = pl.ds(part * CHUNK, CHUNK)
-        mine = pl.ds(HALO + block * ROWS + part * CHUNK, CHUNK)
+            grad_left(q, {"sky": sky + 1}).wait_recv()
+            acc[mine(q), COLS : COLS + PAD] += edge_in[1, flat(q), :].astype(jnp.float32)
+
+    def reduce_down(q, where):
+        return remote(send_r.at[flat(q)], recv_r.at[flat(q)], rs_r_send.at[q], rs_r_recv.at[q], where)
+
+    def reduce_up(q, where):
+        return remote(send_l.at[flat(q)], recv_l.at[flat(q)], rs_l_send.at[q], rs_l_recv.at[q], where)
+
+    def pass_on(q, down):
         staged, arrived = (send_r, recv_r) if down else (send_l, recv_l)
         move = reduce_down if down else reduce_up
         fed = has_up if down else has_down
@@ -439,44 +442,83 @@
 
         @pl.when(fed)
         def _():
-            move(block, part, in_from).wait_recv()
-            staged[block, rows] = (
-                acc[mine, PAD : PAD + COLS] + arrived[block, rows].astype(jnp.float32)
+            move(q, in_from).wait_recv()
+            staged[flat(q), :] = (
+                acc[mine(q), PAD : PAD + COLS] + arrived[flat(q), :].astype(jnp.float32)
             ).astype(jnp.bfloat16)
 
         @pl.when(jnp.logical_not(fed))
         def _():
-            staged[block, rows] = acc[mine, PAD : PAD + COLS].astype(jnp.bfloat16)
-
-        move(block, part, out_to).start()
-
-    for block in order:
-        merge_edges(block)
-    for k in range(n - 1):
-        down_block, up_block = n - 1 - k, k
-        for part in range(PARTS):
-            @pl.when(me < down_block)
-            def _():
-                pass_on(down_block, part, True)
-
-            @pl.when(me > up_block)
-            def _():
-                pass_on(up_block, part, False)
+            staged[flat(q), :] = acc[mine(q), PAD : PAD + COLS].astype(jnp.bfloat16)
+
+        move(q, out_to).start()
+
+    def pass_far(i):
+        merge(far(i))
+
+        @pl.when(upper)
+        def _():
+            pass_on(far(i), True)
+
+        @pl.when(jnp.logical_not(upper))
+        def _():
+            pass_on(far(i), False)
+
+    inner = (me > 0) & (me < n - 1)
+
+    def pass_near(j):
+        merge(near(j))
+        inward = upper != inner
+
+        @pl.when(inward)
+        def _():
+            pass_on(near(j), True)
+
+        @pl.when(jnp.logical_not(inward))
+        def _():
+            pass_on(near(j), False)
+
+    for j in range(half_pieces - 1):
+        share(near(j))
+    for i in range(half_pieces):
+        compute(far(i), 0)
+        if i >= 1:
+            share(far(i - 1))
+        if i >= 2:
+            pass_far(i - 2)
+    share(far(half_pieces - 1))
+    share(near(half_pieces - 1))
+    for i in range(half_pieces - 2, PARTS):
+        pass_far(i)
+
+    @pl.when(inner)
+    def _():
+        for j in range(PARTS):
+            pass_near(j)
+
+    for i in range(max(PARTS, half_pieces - 2), half_pieces):
+        pass_far(i)
+
+    @pl.when(jnp.logical_not(inner))
+    def _():
+        for j in range(PARTS, half_pieces):
+            pass_near(j)
 
     for part in range(PARTS):
         rows = pl.ds(part * CHUNK, CHUNK)
-        mine = pl.ds(pl.multiple_of(HALO + me * ROWS + part * CHUNK, HALO), CHUNK)
-        out_ref[rows, :] = acc[mine, PAD : PAD + COLS]
+        q = me * PARTS + part
+        merge(q)
+        out_ref[rows, :] = acc[mine(q), PAD : PAD + COLS]
 
         @pl.when(has_up)
         def _():
-            reduce_down(me, part, {"epoch": me - 1}).wait_recv()
-            out_ref[rows, :] += recv_r[me, rows].astype(jnp.float32)
+            reduce_down(q, {"epoch": me - 1}).wait_recv()
+            out_ref[rows, :] += recv_r[flat(q), :].astype(jnp.float32)
 
         @pl.when(has_down)
         def _():
-            reduce_up(me, part, {"epoch": me + 1}).wait_recv()
-            out_ref[rows, :] += recv_l[me, rows].astype(jnp.float32)
+            reduce_up(q, {"epoch": me + 1}).wait_recv()
+            out_ref[rows, :] += recv_l[flat(q), :].astype(jnp.float32)
 
     for t in range(n - 1):
         for part in range(PARTS):
@@ -487,24 +529,30 @@
             @pl.when(has_up & (me + t <= n - 1))
             def _():
                 gather_up(t, part).wait_send()
-
-            @pl.when(me < n - 1 - t)
-            def _():
-                reduce_down(n - 1 - t, part, {"epoch": me + 1}).wait_send()
-
-            @pl.when(me > t)
-            def _():
-                reduce_up(t, part, {"epoch": me - 1}).wait_send()
+    for q in range(pieces):
+        @pl.when(me < q // PARTS)
+        def _():
+            reduce_down(q, {"epoch": me + 1}).wait_send()
+
+        @pl.when(me > q // PARTS)
+        def _():
+            reduce_up(q, {"epoch": me - 1}).wait_send()
+
+        @pl.when(has_right)
+        def _():
+            grad_right(q, {"sky": sky + 1}).wait_send()
+
+        @pl.when(has_left)
+        def _():
+            grad_left(q, {"sky": sky - 1}).wait_send()
     for block in range(n):
         @pl.when(has_right)
         def _():
             sky_right(block).wait_send()
-            grad_right(block, {"sky": sky + 1}).wait_send()
 
         @pl.when(has_left)
         def _():
             sky_left(block).wait_send()
-            grad_left(block, {"sky": sky - 1}).wait_send()
 
 
 def fused_plan(sky_scene, images, psf_rows, psf_cols, offsets, epoch_weight, column_mask, coverage):
@@ -535,19 +583,18 @@
             pltpu.VMEM((CHUNK, WIDE), bf),
             pltpu.VMEM((CHUNK, COLS), bf),
             pltpu.VMEM((2, local * SUB, WIDE), bf),
-            pltpu.VMEM((2, n, ROWS, PAD), bf),
-            pltpu.VMEM((2, n, ROWS, PAD), bf),
-            pltpu.VMEM((n, ROWS, COLS), bf),
-            pltpu.VMEM((n, ROWS, COLS), bf),
-            pltpu.VMEM((n, ROWS, COLS), bf),
-            pltpu.VMEM((n, ROWS, COLS), bf),
+            pltpu.VMEM((2, total, PAD), bf),
+            pltpu.VMEM((2, total, PAD), bf),
+            pltpu.VMEM((total, COLS), bf),
+            pltpu.VMEM((total, COLS), bf),
+            pltpu.VMEM((total, COLS), bf),
+            pltpu.VMEM((total, COLS), bf),
             dma,
             dma((local,)),
         ]
         + [dma((n, PARTS))] * 4
         + [dma((n,))] * 4
-        + [dma((n, PARTS))] * 4
-        + [dma((n,))] * 4,
+        + [dma((n * PARTS,))] * 8,
         compiler_params=pltpu.CompilerParams(
             collective_id=0, has_side_effects=True, vmem_limit_bytes=48 << 20
         ),
@@ -557,7 +604,7 @@
 def on_device(sky_scene, images, *rest):
     n = lax.axis_size("epoch")
     fits = (
-        2 <= n <= 4
+        n == 4
         and sky_scene.shape == (ROWS, COLS)
         and images.shape[1:] == (n * ROWS, COLS)
         and images.shape[0] <= 2

time: 109 us -> 91.1 us (0.84)
  the two profiles are of different devices: /device:TPU:18 before, /device:TPU:17 now
where the time goes in v2:
time: 91.1 us; the launch traced here: 90.7 us
  Pallas kernels  82.7 us (91%)
  local copies, waits for them, and re-layouts  5.75 us (6%)
  other arithmetic  2.2 us (2%)
    pallas_call x1, Pallas kernels, fused_plan(): pl.pallas_call(functools.partial(fused_kernel, n, sky_count, taps, local)...  82.7 us
    unnamed x8, local copies, waits for them, and re-layouts  5.67 us

profile of v2, /device:TPU:17, one launch (start us, length us, event | category | flops | bytes accessed | tf_op | source)
XLA Modules:
  0.0 90.7 jit_solution(13490611849479757690)
XLA Ops:
  0.0 0.7 broadcast_multiply_fusion.1
  0.7 0.7 dynamic-slice_convert_fusion
  1.4 0.1 copy.9
  1.4 0.1 broadcast_multiply_fusion.factor_ref
  1.5 0.8 maximum_convert_fusion.psf_ref
  2.3 0.8 copy.10.offset_ref
  3.0 0.0 copy-start
  3.0 2.2 %copy-done = bf16[2,2048,512]{2,1,0:T(8,128)(2,1)S(1)} copy-done((bf16[2,2048,512]{2,1,0:T(8,128)(2,1)S(1)}, bf16[2,2048,512]{2,1,0:T(8,128)(2,1)}, u32[]{:S(2)}) %copy-start) | copy-done | bytes 4194328
  5.2 0.0 copy-start.1
  5.2 1.0 %copy-done.1 = bf16[512,512]{1,0:T(8,128)(2,1)S(1)} copy-done((bf16[512,512]{1,0:T(8,128)(2,1)S(1)}, bf16[512,512]{1,0:T(8,128)(2,1)}, u32[]{:S(2)}) %copy-start.1) | copy-done | bytes 524312
  6.3 0.0 copy-start.2
  6.3 0.7 copy-done.2
  7.0 82.7 %shard_map.82 = f32[512,512]{1,0:T(8,128)S(1)} custom-call(f32[8,50]{1,0:T(8,128)S(1)} %maximum_convert_fusion.psf_ref, s32[8,2]{1,0:T(8,128)S(1)} %copy.10.offset_ref, f32[8,4]{1,0:T(8,128)S(1)} %broadcast_multiply_fusion.factor_ref, s32[8,512]{1,0:T(8,128)S(1)} %copy-done.2, bf16[512,512]{1,0:T(8,128)(2,1)S(1)} %copy-done.1, bf16[2,2048,512]{2,1,0:T(8,128)(2,1)S(1)} %copy-done), custom_call_target="tpu_custom_call" | custom-call | tf_op jit(solution)/shard_map/pallas_call | solution.py:571
  89.7 1.0 %copy.12 = f32[512,512]{1,0:T(8,128)} copy(f32[512,512]{1,0:T(8,128)S(1)} %shard_map.82) | data formatting | bytes 2097152
Async XLA Ops:
  3.0 2.2 %copy-start = (bf16[2,2048,512]{2,1,0:T(8,128)(2,1)S(1)}, bf16[2,2048,512]{2,1,0:T(8,128)(2,1)}, u32[]{:S(2)}) copy-start(bf16[2,2048,512]{2,1,0:T(8,128)(2,1)} %image_ref.1) | copy-start | bytes 12582916
  5.2 1.0 %copy-start.1 = (bf16[512,512]{1,0:T(8,128)(2,1)S(1)}, bf16[512,512]{1,0:T(8,128)(2,1)}, u32[]{:S(2)}) copy-start(bf16[512,512]{1,0:T(8,128)(2,1)} %scene_ref.1) | copy-start | bytes 1572868
  6.3 0.7 copy-start.2

commit v3 on v2

--- a/solution.py
+++ b/solution.py
@@ -129,10 +129,10 @@
 
 def fused_kernel(
     n, sky_count, taps, local,
-    psf_ref, offset_ref, factor_ref, mask_ref, scene_ref, image_ref, out_ref,
-    strip, acc, image_buf, row_tab, rowt_tab, col_tab, lift, res, pull,
+    psf_ref, mask_in, scene_ref, image_ref, out_ref,
+    strip, acc, image_buf, mask_ref, row_tab, rowt_tab, col_tab, lift, res, pull,
     edge_out, edge_in, send_r, recv_r, send_l, recv_l,
-    load_sem, image_sem,
+    load_sem, image_sem, mask_sem,
     ag_r_send, ag_r_recv, ag_l_send, ag_l_recv,
     sky_r_send, sky_r_recv, sky_l_send, sky_l_recv,
     rs_r_send, rs_r_recv, rs_l_send, rs_l_recv,
@@ -154,6 +154,8 @@
     centre = pl.ds(PAD, COLS)
     load = pltpu.make_async_copy(scene_ref, strip.at[rows_of(me), centre], load_sem)
     load.start()
+    mask_load = pltpu.make_async_copy(mask_in, mask_ref, mask_sem)
+    mask_load.start()
     image_loads = [
         pltpu.make_async_copy(image_ref.at[e], image_buf.at[e], image_sem.at[e])
         for e in range(local)
@@ -267,8 +269,8 @@
     lax.fori_loop(0, (total + 2 * HALO) // 32, clear, 0)
 
     for e in range(local):
-        shift_r = offset_ref[base + e, 0]
-        shift_c = offset_ref[base + e, 1]
+        shift_r = psf_ref[base + e, 2 * taps].astype(jnp.int32)
+        shift_c = psf_ref[base + e, 2 * taps + 1].astype(jnp.int32)
         out_i = lax.broadcasted_iota(jnp.int32, (SUB, REACH), 0)
         in_i = lax.broadcasted_iota(jnp.int32, (SUB, REACH), 1)
         row_tab[e] = band(in_i - out_i - HALO - shift_r + half, psf_ref, base + e, 0, taps)
@@ -296,7 +298,7 @@
                 lift[u * SUB : (u + 1) * SUB, :] = jnp.dot(
                     row_tab[e], window, preferred_element_type=jnp.float32
                 ).astype(jnp.bfloat16)
-            factor = factor_ref[base + e, q // PARTS] * mask_ref[pl.ds(base + e, 1), :].astype(
+            factor = psf_ref[base + e, 2 * taps + 2 + q // PARTS] * mask_ref[pl.ds(base + e, 1), :].astype(
                 jnp.float32
             )
             for h in range(2):
@@ -327,6 +329,7 @@
             acc[where, :] += jnp.dot(rowt_tab[...], pull[u], preferred_element_type=jnp.float32)
         return carry
 
+    mask_load.wait()
     for copy in image_loads:
         copy.wait()
     wait_edges(me)
@@ -340,6 +343,100 @@
         first = jnp.where(low == 0, 0, low + 1)
         stop = jnp.where(high == n - 1, n, high)
         return jnp.maximum(first, near_low), jnp.minimum(stop, near_low + n // 2)
+
+    pieces = n * PARTS
+    half_pieces = pieces // 2
+
+    def far(i):
+        return jnp.where(upper, pieces - 1 - i, i)
+
+    def near(j):
+        return jnp.where(upper, j, pieces - 1 - j)
+
+    def flat(q):
+        return pl.ds(pl.multiple_of(q * CHUNK, CHUNK), CHUNK)
+
+    def mine(q):
+        return pl.ds(pl.multiple_of(HALO + q * CHUNK, HALO), CHUNK)
+
+    def grad_right(q, where):
+        return remote(edge_out.at[1, flat(q)], edge_in.at[0, flat(q)], ed_r_send.at[q], ed_r_recv.at[q], where)
+
+    def grad_left(q, where):
+        return remote(edge_out.at[0, flat(q)], edge_in.at[1, flat(q)], ed_l_send.at[q], ed_l_recv.at[q], where)
+
+    def share(q):
+        @pl.when(has_right)
+        def _():
+            edge_out[1, flat(q), :] = acc[mine(q), PAD + COLS : WIDE].astype(jnp.bfloat16)
+            grad_right(q, {"sky": sky + 1}).start()
+
+        @pl.when(has_left)
+        def _():
+            edge_out[0, flat(q), :] = acc[mine(q), 0:PAD].astype(jnp.bfloat16)
+            grad_left(q, {"sky": sky - 1}).start()
+
+    def merge(q):
+        @pl.when(has_left)
+        def _():
+            grad_right(q, {"sky": sky - 1}).wait_recv()
+            acc[mine(q), PAD : 2 * PAD] += edge_in[0, flat(q), :].astype(jnp.float32)
+
+        @pl.when(has_right)
+        def _():
+            grad_left(q, {"sky": sky + 1}).wait_recv()
+            acc[mine(q), COLS : COLS + PAD] += edge_in[1, flat(q), :].astype(jnp.float32)
+
+    def reduce_down(q, where):
+        return remote(send_r.at[flat(q)], recv_r.at[flat(q)], rs_r_send.at[q], rs_r_recv.at[q], where)
+
+    def reduce_up(q, where):
+        return remote(send_l.at[flat(q)], recv_l.at[flat(q)], rs_l_send.at[q], rs_l_recv.at[q], where)
+
+    def pass_on(q, down):
+        staged, arrived = (send_r, recv_r) if down else (send_l, recv_l)
+        move = reduce_down if down else reduce_up
+        fed = has_up if down else has_down
+        out_to = {"epoch": me + 1} if down else {"epoch": me - 1}
+        in_from = {"epoch": me - 1} if down else {"epoch": me + 1}
+
+        @pl.when(fed)
+        def _():
+            move(q, in_from).wait_recv()
+            staged[flat(q), :] = (
+                acc[mine(q), PAD : PAD + COLS] + arrived[flat(q), :].astype(jnp.float32)
+            ).astype(jnp.bfloat16)
+
+        @pl.when(jnp.logical_not(fed))
+        def _():
+            staged[flat(q), :] = acc[mine(q), PAD : PAD + COLS].astype(jnp.bfloat16)
+
+        move(q, out_to).start()
+
+    def pass_far(i):
+        merge(far(i))
+
+        @pl.when(upper)
+        def _():
+            pass_on(far(i), True)
+
+        @pl.when(jnp.logical_not(upper))
+        def _():
+            pass_on(far(i), False)
+
+    inner = (me > 0) & (me < n - 1)
+
+    def pass_near(j):
+        merge(near(j))
+        inward = upper != inner
+
+        @pl.when(inward)
+        def _():
+            pass_on(near(j), True)
+
+        @pl.when(jnp.logical_not(inward))
+        def _():
+            pass_on(near(j), False)
 
     for t in range(n - 1):
         for part in range(PARTS):
@@ -383,111 +480,35 @@
             def _():
                 block = jnp.where(upper, 1, n - 2)
                 lax.fori_loop(block * PARTS, (block + 1) * PARTS, compute, 0)
-
-    pieces = n * PARTS
-    half_pieces = pieces // 2
-
-    def far(i):
-        return jnp.where(upper, pieces - 1 - i, i)
-
-    def near(j):
-        return jnp.where(upper, j, pieces - 1 - j)
-
-    def flat(q):
-        return pl.ds(pl.multiple_of(q * CHUNK, CHUNK), CHUNK)
-
-    def mine(q):
-        return pl.ds(pl.multiple_of(HALO + q * CHUNK, HALO), CHUNK)
-
-    def grad_right(q, where):
-        return remote(edge_out.at[1, flat(q)], edge_in.at[0, flat(q)], ed_r_send.at[q], ed_r_recv.at[q], where)
-
-    def grad_left(q, where):
-        return remote(edge_out.at[0, flat(q)], edge_in.at[1, flat(q)], ed_l_send.at[q], ed_l_recv.at[q], where)
-
-    def share(q):
-        @pl.when(has_right)
-        def _():
-            edge_out[1, flat(q), :] = acc[mine(q), PAD + COLS : WIDE].astype(jnp.bfloat16)
-            grad_right(q, {"sky": sky + 1}).start()
-
-        @pl.when(has_left)
-        def _():
-            edge_out[0, flat(q), :] = acc[mine(q), 0:PAD].astype(jnp.bfloat16)
-            grad_left(q, {"sky": sky - 1}).start()
-
-    def merge(q):
-        @pl.when(has_left)
-        def _():
-            grad_right(q, {"sky": sky - 1}).wait_recv()
-            acc[mine(q), PAD : 2 * PAD] += edge_in[0, flat(q), :].astype(jnp.float32)
-
-        @pl.when(has_right)
-        def _():
-            grad_left(q, {"sky": sky + 1}).wait_recv()
-            acc[mine(q), COLS : COLS + PAD] += edge_in[1, flat(q), :].astype(jnp.float32)
-
-    def reduce_down(q, where):
-        return remote(send_r.at[flat(q)], recv_r.at[flat(q)], rs_r_send.at[q], rs_r_recv.at[q], where)
-
-    def reduce_up(q, where):
-        return remote(send_l.at[flat(q)], recv_l.at[flat(q)], rs_l_send.at[q], rs_l_recv.at[q], where)
-
-    def pass_on(q, down):
-        staged, arrived = (send_r, recv_r) if down else (send_l, recv_l)
-        move = reduce_down if down else reduce_up
-        fed = has_up if down else has_down
-        out_to = {"epoch": me + 1} if down else {"epoch": me - 1}
-        in_from = {"epoch": me - 1} if down else {"epoch": me + 1}
-
-        @pl.when(fed)
-        def _():
-            move(q, in_from).wait_recv()
-            staged[flat(q), :] = (
-                acc[mine(q), PAD : PAD + COLS] + arrived[flat(q), :].astype(jnp.float32)
-            ).astype(jnp.bfloat16)
-
-        @pl.when(jnp.logical_not(fed))
-        def _():
-            staged[flat(q), :] = acc[mine(q), PAD : PAD + COLS].astype(jnp.bfloat16)
-
-        move(q, out_to).start()
-
-    def pass_far(i):
-        merge(far(i))
-
-        @pl.when(upper)
-        def _():
-            pass_on(far(i), True)
-
-        @pl.when(jnp.logical_not(upper))
-        def _():
-            pass_on(far(i), False)
-
-    inner = (me > 0) & (me < n - 1)
-
-    def pass_near(j):
-        merge(near(j))
-        inward = upper != inner
-
-        @pl.when(inward)
-        def _():
-            pass_on(near(j), True)
-
-        @pl.when(jnp.logical_not(inward))
-        def _():
-            pass_on(near(j), False)
-
-    for j in range(half_pieces - 1):
-        share(near(j))
+                for j in range(half_pieces - 1):
+                    share(near(j))
+                compute(far(half_pieces - 1), 0)
+                share(near(half_pieces - 1))
+                for j in range(PARTS, half_pieces):
+                    pass_near(j)
+
+    @pl.when(inner)
+    def _():
+        for j in range(half_pieces - 1):
+            share(near(j))
+
     for i in range(half_pieces):
-        compute(far(i), 0)
+        if i < half_pieces - 1:
+            compute(far(i), 0)
+        else:
+            @pl.when(inner)
+            def _():
+                compute(far(i), 0)
         if i >= 1:
             share(far(i - 1))
         if i >= 2:
             pass_far(i - 2)
     share(far(half_pieces - 1))
-    share(near(half_pieces - 1))
+
+    @pl.when(inner)
+    def _():
+        share(near(half_pieces - 1))
+
     for i in range(half_pieces - 2, PARTS):
         pass_far(i)
 
@@ -498,11 +519,6 @@
 
     for i in range(max(PARTS, half_pieces - 2), half_pieces):
         pass_far(i)
-
-    @pl.when(jnp.logical_not(inner))
-    def _():
-        for j in range(PARTS, half_pieces):
-            pass_near(j)
 
     for part in range(PARTS):
         rows = pl.ds(part * CHUNK, CHUNK)
@@ -559,11 +575,13 @@
     n, sky_count = lax.axis_size("epoch"), lax.axis_size("sky")
     local, total = images.shape[0], images.shape[1]
     taps = psf_rows.shape[1]
-    psf = jnp.concatenate([psf_rows, psf_cols], axis=1).astype(jnp.float32)
     tile_column = lax.axis_index("sky") * COLS // TILE
     tiles = lax.dynamic_index_in_dim(coverage, tile_column, 2, keepdims=False)
     factor = 2.0 * epoch_weight[:, None] * tiles.astype(jnp.float32)
     bf, f32 = jnp.bfloat16, jnp.float32
+    scalars = jnp.concatenate(
+        [value.astype(f32) for value in (psf_rows, psf_cols, offsets, factor)], axis=1
+    )
     smem = pl.BlockSpec(memory_space=pltpu.SMEM)
     vmem = pl.BlockSpec(memory_space=pltpu.VMEM)
     anywhere = pl.BlockSpec(memory_space=pl.ANY)
@@ -571,12 +589,13 @@
     return pl.pallas_call(
         functools.partial(fused_kernel, n, sky_count, taps, local),
         out_shape=jax.ShapeDtypeStruct((ROWS, COLS), f32),
-        in_specs=[smem, smem, smem, vmem, anywhere, anywhere],
+        in_specs=[smem, anywhere, anywhere, anywhere],
         out_specs=vmem,
         scratch_shapes=[
             pltpu.VMEM((total + 2 * HALO, WIDE), bf),
             pltpu.VMEM((total + 2 * HALO, WIDE), f32),
             pltpu.VMEM((local, total, COLS), bf),
+            pltpu.VMEM(column_mask.shape, jnp.int32),
             pltpu.VMEM((local, SUB, REACH), bf),
             pltpu.VMEM((REACH, local * SUB), bf),
             pltpu.VMEM((local, 512, 256), bf),
@@ -591,6 +610,7 @@
             pltpu.VMEM((total, COLS), bf),
             dma,
             dma((local,)),
+            dma,
         ]
         + [dma((n, PARTS))] * 4
         + [dma((n,))] * 4
@@ -598,7 +618,7 @@
         compiler_params=pltpu.CompilerParams(
             collective_id=0, has_side_effects=True, vmem_limit_bytes=48 << 20
         ),
-    )(psf, offsets, factor, column_mask, sky_scene, images)
+    )(scalars, column_mask, sky_scene, images)
 
 
 def on_device(sky_scene, images, *rest):

time: 91.1 us -> 92.3 us (1.013)
  no operation moved by 1% of the time
where the time goes in v3:
time: 92.3 us; the launch traced here: 91.7 us
  Pallas kernels  83 us (90%)
  local copies, waits for them, and re-layouts  5.76 us (6%)
  other arithmetic  2.88 us (3%)
    pallas_call x1, Pallas kernels, fused_plan(): pl.pallas_call(functools.partial(fused_kernel, n, sky_count, taps, local)...  83 us
    unnamed x8, local copies, waits for them, and re-layouts  5.67 us

profile of v3, /device:TPU:17, one launch (start us, length us, event | category | flops | bytes accessed | tf_op | source)
XLA Modules:
  0.0 91.7 jit_solution(11055084470704608951)
XLA Ops:
  0.0 0.7 broadcast_multiply_fusion.1
  0.7 0.7 dynamic-slice_convert_fusion
  1.4 0.1 copy.10
  1.4 0.1 broadcast_multiply_fusion
  1.5 0.7 convert_element_type.15
  2.2 0.7 convert_element_type.16
  2.9 0.8 copy.9
  3.6 0.1 pad_maximum_fusion.psf_ref
  3.7 0.0 copy-start
  3.7 2.2 %copy-done = bf16[2,2048,512]{2,1,0:T(8,128)(2,1)S(1)} copy-done((bf16[2,2048,512]{2,1,0:T(8,128)(2,1)S(1)}, bf16[2,2048,512]{2,1,0:T(8,128)(2,1)}, u32[]{:S(2)}) %copy-start) | copy-done | bytes 4194328
  5.9 0.0 copy-start.1
  5.9 1.0 %copy-done.1 = bf16[512,512]{1,0:T(8,128)(2,1)S(1)} copy-done((bf16[512,512]{1,0:T(8,128)(2,1)S(1)}, bf16[512,512]{1,0:T(8,128)(2,1)}, u32[]{:S(2)}) %copy-start.1) | copy-done | bytes 524312
  7.0 0.0 copy-start.2
  7.0 0.7 copy-done.2
  7.7 83.0 %shard_map.82 = f32[512,512]{1,0:T(8,128)S(1)} custom-call(f32[8,56]{1,0:T(8,128)S(1)} %pad_maximum_fusion.psf_ref, s32[8,512]{1,0:T(8,128)S(1)} %copy-done.2, bf16[512,512]{1,0:T(8,128)(2,1)S(1)} %copy-done.1, bf16[2,2048,512]{2,1,0:T(8,128)(2,1)S(1)} %copy-done), custom_call_target="tpu_custom_call" | custom-call | tf_op jit(solution)/shard_map/pallas_call | solution.py:589
  90.7 1.0 %copy.12 = f32[512,512]{1,0:T(8,128)} copy(f32[512,512]{1,0:T(8,128)S(1)} %shard_map.82) | data formatting | bytes 2097152
  (1 shorter events, 0.0 us)
Async XLA Ops:
  3.7 2.2 %copy-start = (bf16[2,2048,512]{2,1,0:T(8,128)(2,1)S(1)}, bf16[2,2048,512]{2,1,0:T(8,128)(2,1)}, u32[]{:S(2)}) copy-start(bf16[2,2048,512]{2,1,0:T(8,128)(2,1)} %image_ref.1) | copy-start | bytes 12582916
  5.9 1.0 %copy-start.1 = (bf16[512,512]{1,0:T(8,128)(2,1)S(1)}, bf16[512,512]{1,0:T(8,128)(2,1)}, u32[]{:S(2)}) copy-start(bf16[512,512]{1,0:T(8,128)(2,1)} %scene_ref.1) | copy-start | bytes 1572868
  7.0 0.7 copy-start.2

commit v4 on v2

--- a/solution.py
+++ b/solution.py
@@ -129,10 +129,10 @@
 
 def fused_kernel(
     n, sky_count, taps, local,
-    psf_ref, offset_ref, factor_ref, mask_ref, scene_ref, image_ref, out_ref,
-    strip, acc, image_buf, row_tab, rowt_tab, col_tab, lift, res, pull,
+    psf_ref, offset_ref, factor_ref, mask_in, scene_ref, image_ref, out_ref,
+    strip, acc, image_buf, mask_ref, row_tab, rowt_tab, col_tab, lift, res, pull,
     edge_out, edge_in, send_r, recv_r, send_l, recv_l,
-    load_sem, image_sem,
+    load_sem, image_sem, mask_sem,
     ag_r_send, ag_r_recv, ag_l_send, ag_l_recv,
     sky_r_send, sky_r_recv, sky_l_send, sky_l_recv,
     rs_r_send, rs_r_recv, rs_l_send, rs_l_recv,
@@ -154,6 +154,8 @@
     centre = pl.ds(PAD, COLS)
     load = pltpu.make_async_copy(scene_ref, strip.at[rows_of(me), centre], load_sem)
     load.start()
+    mask_load = pltpu.make_async_copy(mask_in, mask_ref, mask_sem)
+    mask_load.start()
     image_loads = [
         pltpu.make_async_copy(image_ref.at[e], image_buf.at[e], image_sem.at[e])
         for e in range(local)
@@ -327,6 +329,7 @@
             acc[where, :] += jnp.dot(rowt_tab[...], pull[u], preferred_element_type=jnp.float32)
         return carry
 
+    mask_load.wait()
     for copy in image_loads:
         copy.wait()
     wait_edges(me)
@@ -566,17 +569,18 @@
     bf, f32 = jnp.bfloat16, jnp.float32
     smem = pl.BlockSpec(memory_space=pltpu.SMEM)
     vmem = pl.BlockSpec(memory_space=pltpu.VMEM)
-    anywhere = pl.BlockSpec(memory_space=pl.ANY)
+    anywhere = pl.BlockSpec(memory_space=pltpu.HBM)
     dma = pltpu.SemaphoreType.DMA
     return pl.pallas_call(
         functools.partial(fused_kernel, n, sky_count, taps, local),
         out_shape=jax.ShapeDtypeStruct((ROWS, COLS), f32),
-        in_specs=[smem, smem, smem, vmem, anywhere, anywhere],
+        in_specs=[smem, smem, smem, anywhere, anywhere, anywhere],
         out_specs=vmem,
         scratch_shapes=[
             pltpu.VMEM((total + 2 * HALO, WIDE), bf),
             pltpu.VMEM((total + 2 * HALO, WIDE), f32),
             pltpu.VMEM((local, total, COLS), bf),
+            pltpu.VMEM(column_mask.shape, jnp.int32),
             pltpu.VMEM((local, SUB, REACH), bf),
             pltpu.VMEM((REACH, local * SUB), bf),
             pltpu.VMEM((local, 512, 256), bf),
@@ -591,6 +595,7 @@
             pltpu.VMEM((total, COLS), bf),
             dma,
             dma((local,)),
+            dma,
         ]
         + [dma((n, PARTS))] * 4
         + [dma((n,))] * 4

time: 91.1 us -> 91.1 us (level)
  no operation moved by 1% of the time
where the time goes in v4:
time: 91.1 us; the launch traced here: 90.7 us
  Pallas kernels  82.8 us (91%)
  local copies, waits for them, and re-layouts  5.75 us (6%)
  other arithmetic  2.2 us (2%)
    pallas_call x1, Pallas kernels, fused_plan(): pl.pallas_call(functools.partial(fused_kernel, n, sky_count, taps, local)...  82.8 us
    unnamed x8, local copies, waits for them, and re-layouts  5.67 us

profile of v4, /device:TPU:17, one launch (start us, length us, event | category | flops | bytes accessed | tf_op | source)
XLA Modules:
  0.0 90.7 jit_solution(9709212252588285192)
XLA Ops:
  0.0 0.7 broadcast_multiply_fusion.1
  0.7 0.7 dynamic-slice_convert_fusion
  1.4 0.1 copy.9
  1.4 0.1 broadcast_multiply_fusion.factor_ref
  1.5 0.8 maximum_convert_fusion.psf_ref
  2.3 0.8 copy.10.offset_ref
  3.0 0.0 copy-start
  3.0 2.2 %copy-done = bf16[2,2048,512]{2,1,0:T(8,128)(2,1)S(1)} copy-done((bf16[2,2048,512]{2,1,0:T(8,128)(2,1)S(1)}, bf16[2,2048,512]{2,1,0:T(8,128)(2,1)}, u32[]{:S(2)}) %copy-start) | copy-done | bytes 4194328
  5.2 0.0 copy-start.1
  5.2 1.0 %copy-done.1 = bf16[512,512]{1,0:T(8,128)(2,1)S(1)} copy-done((bf16[512,512]{1,0:T(8,128)(2,1)S(1)}, bf16[512,512]{1,0:T(8,128)(2,1)}, u32[]{:S(2)}) %copy-start.1) | copy-done | bytes 524312
  6.3 0.0 copy-start.2
  6.3 0.7 copy-done.2
  7.0 82.8 %shard_map.82 = f32[512,512]{1,0:T(8,128)S(1)} custom-call(f32[8,50]{1,0:T(8,128)S(1)} %maximum_convert_fusion.psf_ref, s32[8,2]{1,0:T(8,128)S(1)} %copy.10.offset_ref, f32[8,4]{1,0:T(8,128)S(1)} %broadcast_multiply_fusion.factor_ref, s32[8,512]{1,0:T(8,128)S(1)} %copy-done.2, bf16[512,512]{1,0:T(8,128)(2,1)S(1)} %copy-done.1, bf16[2,2048,512]{2,1,0:T(8,128)(2,1)S(1)} %copy-done), custom_call_target="tpu_custom_call" | custom-call | tf_op jit(solution)/shard_map/pallas_call | solution.py:574
  89.8 1.0 %copy.12 = f32[512,512]{1,0:T(8,128)} copy(f32[512,512]{1,0:T(8,128)S(1)} %shard_map.82) | data formatting | bytes 2097152
Async XLA Ops:
  3.0 2.2 %copy-start = (bf16[2,2048,512]{2,1,0:T(8,128)(2,1)S(1)}, bf16[2,2048,512]{2,1,0:T(8,128)(2,1)}, u32[]{:S(2)}) copy-start(bf16[2,2048,512]{2,1,0:T(8,128)(2,1)} %image_ref.1) | copy-start | bytes 12582916
  5.2 1.0 %copy-start.1 = (bf16[512,512]{1,0:T(8,128)(2,1)S(1)}, bf16[512,512]{1,0:T(8,128)(2,1)}, u32[]{:S(2)}) copy-start(bf16[512,512]{1,0:T(8,128)(2,1)} %scene_ref.1) | copy-start | bytes 1572868
  6.3 0.7 copy-start.2
